TPU v7x, 256 devices: a whole 4x4x8 slice. The times are simulated.
256 devices in a mesh: atoms: 32 (over x_lo, z, core), beads: 8 (over x_hi, y).
Axes of the slice: x: 4 (x_hi: 2, x_lo: 2; x = x_hi * 2 + x_lo), y: 4, z: 8, core: 2. Of those that a mesh axis runs over, the one named last changes fastest.
Arguments:
- positions: float32 [32, 3, 4096], P('beads', None, 'atoms'), may hold values from 0 to 1
- velocities: float32 [32, 3, 4096], P('beads', None, 'atoms'), may hold values from -3 to 3
- charges_in: float32 [32, 4096], P('beads', 'atoms'), may hold values from -3 to 3
- species: int32 [4096], P('atoms'), may hold values from 0 to 7
- neighbors: int32 [8, 4096], P(None, 'atoms'), may hold values from -32 to 32
- k_index: int32 [3, 2048], replicated, may hold values from -8 to 8
- kernel: float32 [2048], replicated, may hold values from 0.1 to 1
- chi_table: float32 [8], replicated, may hold values from -2 to 2
- hard_table: float32 [8], replicated, may hold values from 1 to 4
- bond_table: float32 [8], replicated, may hold values from 0.2 to 0.8
- mass_table: float32 [8], replicated, may hold values from 1 to 8
Outputs:
- new_positions: float32 [32, 3, 4096], P('beads', None, 'atoms')
- new_velocities: float32 [32, 3, 4096], P('beads', None, 'atoms')
- charges: float32 [32, 4096], P('beads', 'atoms')
Inputs may be any that keep to these rules, and one draw needn't show every extreme that they name: species index the tables. `neighbors`: neighbour offsets count in atom order, cyclically over 4096 atoms.
All inputs are finite; a program needn't handle non-finite values.
Results may differ from a plain program's by a relative error of at most 0.00021.
Values sent between devices are 32-bit elements; how exact they have to be, the bound alone decides.
A program may use at most 64 MiB of HBM per device.

v0:
```python
import math
import jax
import jax.numpy as jnp
from jax import lax
from jax.sharding import PartitionSpec as P

KVEC = 2048
QITERS = 2
RIM = 32
SPECIES = 8
two_pi = 2.0 * math.pi
ewald_gain = 4.0
mixing = 0.5
spring_rate = 0.5
time_step = 0.05
HIGH = lax.Precision.HIGHEST


def extended(block, sides, width):
    for axis, dim in sides:
        count = lax.axis_size(axis)
        forward = [(i, i + 1) for i in range(count - 1)]
        forward.append((count - 1, 0))
        backward = [(target, source) for source, target in forward]
        low = lax.ppermute(
            lax.slice_in_dim(block, block.shape[dim] - width, None, axis=dim), axis, forward
        )
        high = lax.ppermute(lax.slice_in_dim(block, 0, width, axis=dim), axis, backward)
        block = jnp.concatenate([low, block, high], axis=dim)
    return block


def phase_tables(positions, nblock):
    angle = two_pi * (
        positions[:, 0, :, None] * nblock[0]
        + positions[:, 1, :, None] * nblock[1]
        + positions[:, 2, :, None] * nblock[2]
    )
    return (jnp.cos(angle), jnp.sin(angle))


def unblock(stacked):
    blocks, beads_here, parts, width = stacked.shape
    return stacked.transpose(1, 2, 0, 3).reshape(beads_here, parts, blocks * width)


def to_blocks(pair, blocks):
    beads_here, parts, total = pair.shape
    return pair.reshape(beads_here, parts, blocks, total // blocks).transpose(2, 0, 1, 3)


def local_factors(positions, charge, wave_blocks):

    def local_visit(unused, nblock):
        cosine, sine_part = phase_tables(positions, nblock)
        real_part = jnp.einsum("ba,bak->bk", charge, cosine, precision=HIGH)
        imag_part = jnp.einsum("ba,bak->bk", charge, sine_part, precision=HIGH)
        pair = jnp.stack([real_part, imag_part], 1)
        return (unused, pair)

    unused, stacked = lax.scan(local_visit, None, wave_blocks)
    return unblock(stacked)


def potential_sum(positions, pair, wave_blocks, kernel_blocks):
    coeff_blocks = to_blocks(pair, wave_blocks.shape[0]) * kernel_blocks[:, None, None, :]

    def potential_visit(accum, inputs):
        nblock, cblock = inputs
        cosine, sine_part = phase_tables(positions, nblock)
        accum = accum + jnp.einsum("bak,bk->ba", cosine, cblock[:, 0], precision=HIGH)
        return (accum + jnp.einsum("bak,bk->ba", sine_part, cblock[:, 1], precision=HIGH), None)

    start = jnp.zeros((positions.shape[0], positions.shape[2]), jnp.float32)
    result, unused = lax.scan(potential_visit, start, (wave_blocks, coeff_blocks))
    return result


def force_sum(positions, pair, wave_blocks, kernel_blocks):
    coeff_blocks = to_blocks(pair, wave_blocks.shape[0]) * kernel_blocks[:, None, None, :]

    def force_visit(accum, inputs):
        nblock, cblock = inputs
        cosine, sine_part = phase_tables(positions, nblock)
        mixed = sine_part * cblock[:, 0][:, None, :] - cosine * cblock[:, 1][:, None, :]
        return (accum + jnp.einsum("bak,dk->bda", mixed, nblock, precision=HIGH), None)

    result, unused = lax.scan(
        force_visit, jnp.zeros(positions.shape, jnp.float32), (wave_blocks, coeff_blocks)
    )
    return result


def summed_factors(positions, charge, wave_blocks):
    return lax.psum(local_factors(positions, charge, wave_blocks), "atoms")


def body(
    positions,
    velocities,
    charges_in,
    species,
    neighbors,
    k_index,
    kernel,
    chi_table,
    hard_table,
    bond_table,
    mass_table,
):
    atom_here = positions.shape[2]
    atom_count = atom_here * lax.axis_size("atoms")
    ewald_scale = ewald_gain / math.sqrt(KVEC * atom_count)
    width = min(256, KVEC)
    blocks = KVEC // width
    wave = k_index.astype(jnp.float32)
    wave_blocks = wave.reshape(3, blocks, width).transpose(1, 0, 2)
    kernel_blocks = kernel.reshape(blocks, width)
    onehot = (species[None, :] == jnp.arange(SPECIES, dtype=jnp.int32)[:, None]).astype(jnp.float32)

    def lookup(table):
        return jnp.sum(table[:, None] * onehot, 0)

    electroneg = lookup(chi_table)
    hardness = lookup(hard_table)
    bond_term = lookup(bond_table)
    atom_mass = lookup(mass_table)
    neighbour_index = jnp.arange(atom_here, dtype=jnp.int32)[None, :] + RIM + neighbors
    charge = charges_in
    for rounds in range(QITERS):
        pair = summed_factors(positions, charge, wave_blocks)
        potential = ewald_scale * potential_sum(positions, pair, wave_blocks, kernel_blocks)
        weighted = bond_term[None, :] * charge
        padded = extended(weighted, (("atoms", 1),), RIM)
        neighbour_sum = jnp.sum(padded[:, neighbour_index], 1)
        relaxed = (1.0 - mixing) * charge + mixing * (
            -(electroneg + potential + bond_term * neighbour_sum) / hardness
        )
        charge_sum = lax.psum(jnp.sum(relaxed, 1), "atoms")
        charge = relaxed - (charge_sum / atom_count)[:, None]
    pair = summed_factors(positions, charge, wave_blocks)
    ewald_force = (
        two_pi
        * ewald_scale
        * charge[:, None, :]
        * force_sum(positions, pair, wave_blocks, kernel_blocks)
    )
    padded_beads = extended(positions, (("beads", 0),), 1)
    laplace = 2.0 * positions - padded_beads[:-2] - padded_beads[2:]
    acceleration = ewald_force / atom_mass[None, None, :] - spring_rate * laplace
    new_velocities = velocities + time_step * acceleration
    new_positions = positions + time_step * new_velocities
    return (new_positions, new_velocities, charge)


def solution(mesh):
    return jax.shard_map(
        body,
        mesh=mesh,
        in_specs=(
            P("beads", None, "atoms"),
            P("beads", None, "atoms"),
            P("beads", "atoms"),
            P("atoms"),
            P(None, "atoms"),
            P(),
            P(),
            P(),
            P(),
            P(),
            P(),
        ),
        out_specs=(P("beads", None, "atoms"), P("beads", None, "atoms"), P("beads", "atoms")),
        check_vma=False,
    )
```

profile of v0, /device:TPU:6, one launch (start us, length us, event | category | flops | bytes accessed | tf_op | source)
XLA Modules:
  0.0 944.2 jit_solution(12425092056688733907)
XLA Ops:
  8.2 5.6 collective-permute-start.1
  15.2 40.7 %while.63 = (s32[]{:T(128)}, f32[8,4,2,256]{3,1,2,0:T(4,128)S(1)}, f32[4,3,128]{2,0,1:T(4,128)S(1)}, f32[8,3,256]{2,1,0:T(4,128)S(1)}, f32[4,128]{1,0:T(4,128)S(1)}, /*index=5*/s32[]{:T(128)}, s32[]{:T(128)}, s32[]{}, s32[]{}) while((s32[]{:T(128)}, f32[8,4,2,256]{3,1,2,0:T(4,128)S(1)}, f32[4,3,128]{2,0,1:T(4,128)S(1)}, ...), condition=%wide.region_2.0_spmd, body=%wide.region_1.0_spmd.sunk | while | flops 4720644 | bytes 114821 | solution.py:61
  57.6 2.8 gather_fusion
  60.6 191.0 %all-reduce.4.cloned.1.call-done = f32[4,2,8,256]{3,0,1,2:T(4,128)} async-done(((f32[4,2,8,256]{3,0,1,2:T(4,128)}), f32[4,2,8,256]{3,0,1,2:T(4,128)}) %all-reduce.4.cloned.1.call-update) | async-done | bytes 65552 | tf_op jit(solution)/shard_map/psum | solution.py:95
  252.5 39.9 %while.66 = (s32[]{:T(128)}, f32[4,128]{1,0:T(4,128)S(1)}, f32[4,3,128]{2,0,1:T(4,128)S(1)}, f32[8,3,256]{2,1,0:T(4,128)S(1)}, f32[8,4,2,256]{3,1,2,0:T(4,128)S(1)}, /*index=5*/s32[]{:T(128)}, s32[]{:T(128)}, s32[]{}, s32[]{}) while((s32[]{:T(128)}, f32[4,128]{1,0:T(4,128)S(1)}, f32[4,3,128]{2,0,1:T(4,128)S(1)}, ...), condition=%wide.region_5.6_spmd.clone, body=%wide.region_4.5_spmd.clone.sunk | while | flops 4720133 | bytes 90255 | solution.py:75
  292.5 54.5 %psum.36 = f32[4]{0:T(128)S(1)} all-reduce(f32[4]{0:T(128)S(1)} %get-tuple-element.386), channel_id=1, replica_groups=mesh['atoms'=32,'beads'=8] {'atoms'}, use_global_device_ids=true, to_apply=%region_10.11 | all-reduce | flops 4 | bytes 32 | tf_op jit(solution)/shard_map/psum | solution.py:139
  347.2 3.9 collective-permute-start.3
  351.0 40.7 %while.64 = (s32[]{:T(128)}, f32[8,4,2,256]{3,1,2,0:T(4,128)S(1)}, f32[4,3,128]{2,0,1:T(4,128)S(1)}, f32[8,3,256]{2,1,0:T(4,128)S(1)}, f32[4,128]{1,0:T(4,128)S(1)}, /*index=5*/s32[]{:T(128)}, s32[]{:T(128)}, s32[]{}, s32[]{}) while((s32[]{:T(128)}, f32[8,4,2,256]{3,1,2,0:T(4,128)S(1)}, f32[4,3,128]{2,0,1:T(4,128)S(1)}, ...), condition=%wide.region_12.13_spmd, body=%wide.region_11.12_spmd.sunk | while | flops 4720644 | bytes 114821 | solution.py:61
  392.7 2.8 gather_fusion.1
  395.6 187.4 %all-reduce.6.cloned.1.call-done = f32[4,2,8,256]{3,0,1,2:T(4,128)} async-done(((f32[4,2,8,256]{3,0,1,2:T(4,128)}), f32[4,2,8,256]{3,0,1,2:T(4,128)}) %all-reduce.6.cloned.1.call-update) | async-done | bytes 65552 | tf_op jit(solution)/shard_map/psum | solution.py:95
  583.9 39.9 %while.67 = (s32[]{:T(128)}, f32[4,128]{1,0:T(4,128)S(1)}, f32[4,3,128]{2,0,1:T(4,128)S(1)}, f32[8,3,256]{2,1,0:T(4,128)S(1)}, f32[8,4,2,256]{3,1,2,0:T(4,128)S(1)}, /*index=5*/s32[]{:T(128)}, s32[]{:T(128)}, s32[]{}, s32[]{}) while((s32[]{:T(128)}, f32[4,128]{1,0:T(4,128)S(1)}, f32[4,3,128]{2,0,1:T(4,128)S(1)}, ...), condition=%wide.region_15.16_spmd.clone, body=%wide.region_14.15_spmd.clone.sunk | while | flops 4720133 | bytes 90255 | solution.py:75
  623.9 54.5 %psum.38 = f32[4]{0:T(128)S(1)} all-reduce(f32[4]{0:T(128)S(1)} %get-tuple-element.382), channel_id=1, replica_groups=mesh['atoms'=32,'beads'=8] {'atoms'}, use_global_device_ids=true, to_apply=%region_18.19 | all-reduce | flops 4 | bytes 32 | tf_op jit(solution)/shard_map/psum | solution.py:139
  678.5 40.8 %while.65 = (s32[]{:T(128)}, f32[8,4,2,256]{3,1,2,0:T(4,128)S(1)}, f32[4,3,128]{2,0,1:T(4,128)S(1)}, f32[8,3,256]{2,1,0:T(4,128)S(1)}, f32[4,128]{1,0:T(4,128)S(1)}, /*index=5*/s32[]{:T(128)}, s32[]{:T(128)}, s32[]{}, s32[]{}) while((s32[]{:T(128)}, f32[8,4,2,256]{3,1,2,0:T(4,128)S(1)}, f32[4,3,128]{2,0,1:T(4,128)S(1)}, ...), condition=%wide.region_20.21_spmd, body=%wide.region_19.20_spmd.sunk | while | flops 4720644 | bytes 114821 | solution.py:61
  721.5 4.2 collective-permute-start.5
  725.7 184.5 %all-reduce.8.cloned.1.call-done = f32[4,2,8,256]{3,0,1,2:T(4,128)} async-done(((f32[4,2,8,256]{3,0,1,2:T(4,128)}), f32[4,2,8,256]{3,0,1,2:T(4,128)}) %all-reduce.8.cloned.1.call-update) | async-done | bytes 65552 | tf_op jit(solution)/shard_map/psum | solution.py:95
  911.0 25.9 %while.68 = (s32[]{:T(128)}, f32[4,3,128]{2,1,0:T(4,128)S(1)}, f32[8,3,256]{2,1,0:T(4,128)S(1)}, f32[4,3,128]{2,0,1:T(4,128)S(1)}, f32[8,4,2,256]{3,1,2,0:T(4,128)S(1)}, /*index=5*/s32[]{:T(128)}, s32[]{:T(128)}, s32[]{}, s32[]{}) while((s32[]{:T(128)}, f32[4,3,128]{2,1,0:T(4,128)S(1)}, f32[8,3,256]{2,1,0:T(4,128)S(1)}, ...), condition=%wide.region_23.24_spmd.clone, body=%wide.region_22.23_spmd.clone.sunk | while | flops 5901317 | bytes 87187 | solution.py:88
  911.1 3.1 fusion.210
  914.4 3.1 fusion.210
  917.6 3.1 fusion.210
  920.8 3.1 fusion.210
  924.1 3.1 fusion.210
  927.3 3.1 fusion.210
  930.6 3.1 fusion.210
  933.8 3.1 fusion.210
  (450 shorter events, 211.7 us)
Async XLA Ops:
  7.2 244.4 %all-reduce.4.cloned.1.call-start = ((), (), s32[]{:S(2)}) async-start(), calls=%async_computation | async-start | bytes 131072 | tf_op jit(solution)/shard_map/psum | solution.py:95
  7.2 0.8 copy-start.4
  8.1 49.3 %collective-permute-start = (f32[4,32]{1,0:T(4,128)S(1)}, f32[4,32]{1,0:T(4,128)S(1)}, u32[]{:S(2)}, u32[]{:S(2)}) collective-permute-start(f32[4,32]{1,0:T(4,128)S(1)} %get-tuple-element.430), channel_id=1, source_target_pairs={{0,8},{8,16},{16,24},{24,32},{32,40},{40,48},{48,56},{56,64},{64,7... | collective-permute-start | bytes 1544 | tf_op jit(solution)/shard_map/ppermute | solution.py:25
  8.2 49.3 %collective-permute-start.1 = (f32[4,32]{1,0:T(4,128)S(1)}, f32[4,32]{1,0:T(4,128)S(1)}, u32[]{:S(2)}, u32[]{:S(2)}) collective-permute-start(f32[4,32]{1,0:T(4,128)S(1)} %get-tuple-element.431), channel_id=1, source_target_pairs={{8,0},{16,8},{24,16},{32,24},{40,32},{48,40},{56,48},{64,56},{72,6... | collective-permute-start | bytes 1544 | tf_op jit(solution)/shard_map/ppermute | solution.py:28
  14.6 0.7 copy-start
  56.0 0.6 copy-start.2
  56.0 0.7 copy-start.7
  56.6 526.4 %all-reduce.6.cloned.1.call-start = ((), (), s32[]{:S(2)}) async-start(), calls=%async_computation.1 | async-start | bytes 131072 | tf_op jit(solution)/shard_map/psum | solution.py:95
  56.7 0.7 copy-start.5
  347.2 45.3 %collective-permute-start.2 = (f32[4,32]{1,0:T(4,128)S(1)}, f32[4,32]{1,0:T(4,128)S(1)}, u32[]{:S(2)}, u32[]{:S(2)}) collective-permute-start(f32[4,32]{1,0:T(4,128)S(1)} %get-tuple-element.428), channel_id=1, source_target_pairs={{0,8},{8,16},{16,24},{24,32},{32,40},{40,48},{48,56},{56,64},{64,7... | collective-permute-start | bytes 1544 | tf_op jit(solution)/shard_map/ppermute | solution.py:25
  347.2 45.3 %collective-permute-start.3 = (f32[4,32]{1,0:T(4,128)S(1)}, f32[4,32]{1,0:T(4,128)S(1)}, u32[]{:S(2)}, u32[]{:S(2)}) collective-permute-start(f32[4,32]{1,0:T(4,128)S(1)} %get-tuple-element.429), channel_id=1, source_target_pairs={{8,0},{16,8},{24,16},{32,24},{40,32},{48,40},{56,48},{64,56},{72,6... | collective-permute-start | bytes 1544 | tf_op jit(solution)/shard_map/ppermute | solution.py:28
  391.8 0.6 copy-start.3
  392.4 517.7 %all-reduce.8.cloned.1.call-start = ((), (), s32[]{:S(2)}) async-start(), calls=%async_computation.2 | async-start | bytes 131072 | tf_op jit(solution)/shard_map/psum | solution.py:95
  719.3 0.6 copy-start.8
  719.3 0.6 copy-start.1
  720.0 217.0 %collective-permute-start.4 = (f32[1,3,128]{2,0,1:T(1,128)S(1)}, f32[1,3,128]{2,0,1:T(1,128)S(1)}, u32[]{:S(2)}, u32[]{:S(2)}) collective-permute-start(f32[1,3,128]{2,0,1:T(1,128)S(1)} %get-tuple-element.426), channel_id=1, source_target_pairs={{0,1},{1,2},{2,3},{3,4},{4,5},{5,6},{6,7},{7,0},{8,9},{9,10},{10,1... | collective-permute-start | bytes 4616 | tf_op jit(solution)/shard_map/ppermute | solution.py:25
  721.5 215.5 %collective-permute-start.5 = (f32[1,3,128]{2,0,1:T(1,128)S(1)}, f32[1,3,128]{2,0,1:T(1,128)S(1)}, u32[]{:S(2)}, u32[]{:S(2)}) collective-permute-start(f32[1,3,128]{2,0,1:T(1,128)S(1)} %get-tuple-element.427), channel_id=1, source_target_pairs={{1,0},{2,1},{3,2},{4,3},{5,4},{6,5},{7,6},{0,7},{9,8},{10,9},{11,1... | collective-permute-start | bytes 4616 | tf_op jit(solution)/shard_map/ppermute | solution.py:28
  911.0 26.0 %copy-start.6 = (f32[4,3,128]{2,0,1:T(4,128)S(1)}, f32[4,3,128]{2,0,1:T(4,128)}, u32[]{:S(2)}) copy-start(f32[4,3,128]{2,0,1:T(4,128)} %param.24) | copy-start | bytes 18436
Sparse Core Ops, SparseCore 0:
  56.8 194.7 all-reduce.3
  392.5 190.4 all-reduce.5
  720.1 190.0 all-reduce.7
where the time goes:
time: 945 us; the launch traced here: 944 us
  waiting for transfers between devices  563 us (60%)
  matrix products  223 us (24%)
  blocking collectives  109 us (12%)
  starting transfers between devices  15.4 us (2%)
  between operations  14.1 us (1%)
  local copies, waits for them, and re-layouts  11.7 us (1%)
    psum x3, waiting for transfers between devices, summed_factors(): return lax.psum(local_factors(positions, charge, wave_blocks), 'atoms')  563 us
    psum x2, blocking collectives, body(): charge_sum = lax.psum(jnp.sum(relaxed, 1), 'atoms')  109 us
    dot_general x24, matrix products, local_visit(): imag_part = jnp.einsum('ba,bak->bk', charge, sine_part, precision=HIGH)  59.9 us
    dot_general x24, matrix products, local_visit(): real_part = jnp.einsum('ba,bak->bk', charge, cosine, precision=HIGH)  59.5 us
    dot_general x16, matrix products, potential_visit(): jnp.einsum('bak,bk->ba', sine_part, cblock[:, 1], precision=HIGH)  39.5 us
    dot_general x16, matrix products, potential_visit(): jnp.einsum('bak,bk->ba', cosine, cblock[:, 0], precision=HIGH)  38.8 us
    dot_general x8, matrix products, force_visit(): jnp.einsum('bak,dk->bda', mixed, nblock, precision=HIGH)  25.1 us
  transfers between devices with their start and end apart: 9, of which 3 were waited for; matrix products, arithmetic and copies ran while one was open for 12% of the time, Pallas kernels for 0%

commit v1 on v0

--- a/solution.py
+++ b/solution.py
@@ -14,6 +14,12 @@
 spring_rate = 0.5
 time_step = 0.05
 HIGH = lax.Precision.HIGHEST
+
+
+def gather_and_add(value, name):
+    terms = lax.all_gather(value, name, axis=0, tiled=False)
+    summed = terms.sum(axis=0)
+    return summed
 
 
 def extended(block, sides, width):
@@ -92,7 +98,7 @@
 
 
 def summed_factors(positions, charge, wave_blocks):
-    return lax.psum(local_factors(positions, charge, wave_blocks), "atoms")
+    return gather_and_add(local_factors(positions, charge, wave_blocks), "atoms")
 
 
 def body(

time: 945 us -> 566 us (0.60)
  waiting for transfers between devices: 563 us -> 164 us
    psum x3 -> x0, waiting for transfers between devices: 563 us -> none  [summed_factors(): return lax.psum(local_factors(positions, charge, wave_blocks), 'atoms')]
    all_gather x0 -> x3, waiting for transfers between devices: none -> 162 us  [gather_and_add(): terms = lax.all_gather(value, name, axis=0, tiled=False)]
  transfers between devices with their start and end apart: 9 -> 9, of which waited for: 3 -> 6; matrix products, arithmetic and copies ran while one was open for 12% -> 6% of each run, Pallas kernels for 0% -> 0%
where the time goes in v1:
time: 566 us; the launch traced here: 563 us
  matrix products  230 us (41%)
  waiting for transfers between devices  164 us (29%)
  blocking collectives  111 us (20%)
  local copies, waits for them, and re-layouts  16.3 us (3%)
  starting transfers between devices  15.5 us (3%)
  between operations  14.2 us (3%)
  other arithmetic  9.52 us (2%)
    all_gather x3, waiting for transfers between devices, gather_and_add(): terms = lax.all_gather(value, name, axis=0, tiled=False)  162 us
    psum x2, blocking collectives, body(): charge_sum = lax.psum(jnp.sum(relaxed, 1), 'atoms')  111 us
    dot_general x24, matrix products, local_visit(): imag_part = jnp.einsum('ba,bak->bk', charge, sine_part, precision=HIGH)  63.7 us
    dot_general x24, matrix products, local_visit(): real_part = jnp.einsum('ba,bak->bk', charge, cosine, precision=HIGH)  63.3 us
    dot_general x16, matrix products, potential_visit(): jnp.einsum('bak,bk->ba', sine_part, cblock[:, 1], precision=HIGH)  39.5 us
    dot_general x16, matrix products, potential_visit(): jnp.einsum('bak,bk->ba', cosine, cblock[:, 0], precision=HIGH)  38.8 us
    dot_general x8, matrix products, force_visit(): jnp.einsum('bak,dk->bda', mixed, nblock, precision=HIGH)  25.1 us
    ppermute x3, starting transfers between devices, extended(): lax.ppermute(lax.slice_in_dim(block, 0, width, axis=dim), axis, backward)  13.8 us
  transfers between devices with their start and end apart: 9, of which 6 were waited for; matrix products, arithmetic and copies ran while one was open for 6% of the time, Pallas kernels for 0%

profile of v1, /device:TPU:6, one launch (start us, length us, event | category | flops | bytes accessed | tf_op | source)
XLA Modules:
  0.0 563.2 jit_solution(6706045156608518926)
XLA Ops:
  8.1 53.9 %while.63 = (s32[]{:T(128)}, f32[8,4,2,256]{3,2,1,0:T(2,128)S(1)}, f32[4,3,128]{2,0,1:T(4,128)}, f32[8,3,256]{2,1,0:T(4,128)S(1)}, f32[4,128]{1,0:T(4,128)}, /*index=5*/s32[]{:T(128)}, s32[]{:T(128)}, s32[]{}, s32[]{}) while((s32[]{:T(128)}, f32[8,4,2,256]{3,2,1,0:T(2,128)S(1)}, f32[4,3,128]{2,0,1:T(4,128)}, f32[8,3,256]{2,1,0:T(4,128)S(1)}, ...), condition=%wide.region_2.0_spmd, body=%wide.region_1.0_spmd.sunk | while | flops 4720644 | bytes 98437 | solution.py:67
  11.8 3.0 fusion.193
  18.5 3.0 fusion.193
  63.7 5.8 %collective-permute-start.1 = (f32[4,32]{1,0:T(4,128)S(1)}, f32[4,32]{1,0:T(4,128)S(1)}, u32[]{:S(2)}, u32[]{:S(2)}) collective-permute-start(f32[4,32]{1,0:T(4,128)S(1)} %get-tuple-element.479), channel_id=1, source_target_pairs={{8,0},{16,8},{24,16},{32,24},{40,32},{48,40},{56,48},{64,56},{72,6... | collective-permute-start | bytes 1544 | tf_op jit(solution)/shard_map/ppermute | solution.py:34
  73.9 55.8 %all-gather.4.cloned.1.call-done = f32[32,4,2,2048]{3,1,2,0:T(4,128)} async-done(((f32[1,4,2,2048]{3,1,2,0:T(4,128)}), f32[32,4,2,2048]{3,1,2,0:T(4,128)}) %all-gather.4.cloned.1.call-update) | async-done | bytes 2097168 | tf_op jit(solution)/shard_map/all_gather | solution.py:20
  131.7 39.9 %while.66 = (s32[]{:T(128)}, f32[4,128]{1,0:T(4,128)S(1)}, f32[4,3,128]{2,0,1:T(4,128)S(1)}, f32[8,3,256]{2,1,0:T(4,128)S(1)}, f32[8,4,2,256]{3,0,2,1:T(8,128)S(1)}, /*index=5*/s32[]{:T(128)}, s32[]{:T(128)}, s32[]{}, s32[]{}) while((s32[]{:T(128)}, f32[4,128]{1,0:T(4,128)S(1)}, f32[4,3,128]{2,0,1:T(4,128)S(1)}, ...), condition=%wide.region_5.6_spmd.clone, body=%wide.region_4.5_spmd.clone.sunk | while | flops 4720133 | bytes 90255 | solution.py:81
  171.8 55.5 %psum.14 = f32[4]{0:T(128)S(1)} all-reduce(f32[4]{0:T(128)S(1)} %get-tuple-element.434), channel_id=1, replica_groups=mesh['atoms'=32,'beads'=8] {'atoms'}, use_global_device_ids=true, to_apply=%region_10.11 | all-reduce | flops 4 | bytes 32 | tf_op jit(solution)/shard_map/psum | solution.py:145
  227.4 40.7 %while.64 = (s32[]{:T(128)}, f32[8,4,2,256]{3,2,1,0:T(2,128)S(1)}, f32[4,3,128]{2,0,1:T(4,128)S(1)}, f32[8,3,256]{2,1,0:T(4,128)S(1)}, f32[4,128]{1,0:T(4,128)S(1)}, /*index=5*/s32[]{:T(128)}, s32[]{:T(128)}, s32[]{}, s32[]{}) while((s32[]{:T(128)}, f32[8,4,2,256]{3,2,1,0:T(2,128)S(1)}, f32[4,3,128]{2,0,1:T(4,128)S(1)}, ...), condition=%wide.region_12.13_spmd, body=%wide.region_11.12_spmd.sunk | while | flops 4720644 | bytes 98437 | solution.py:67
  269.0 3.8 collective-permute-start.3
  277.2 51.5 %all-gather.6.cloned.1.call-done = f32[32,4,2,2048]{3,1,2,0:T(4,128)} async-done(((f32[1,4,2,2048]{3,1,2,0:T(4,128)}), f32[32,4,2,2048]{3,1,2,0:T(4,128)}) %all-gather.6.cloned.1.call-update) | async-done | bytes 2097168 | tf_op jit(solution)/shard_map/all_gather | solution.py:20
  330.8 40.0 %while.67 = (s32[]{:T(128)}, f32[4,128]{1,0:T(4,128)S(1)}, f32[4,3,128]{2,0,1:T(4,128)S(1)}, f32[8,3,256]{2,1,0:T(4,128)S(1)}, f32[8,4,2,256]{3,0,2,1:T(8,128)S(1)}, /*index=5*/s32[]{:T(128)}, s32[]{:T(128)}, s32[]{}, s32[]{}) while((s32[]{:T(128)}, f32[4,128]{1,0:T(4,128)S(1)}, f32[4,3,128]{2,0,1:T(4,128)S(1)}, ...), condition=%wide.region_15.16_spmd.clone, body=%wide.region_14.15_spmd.clone.sunk | while | flops 4720133 | bytes 90255 | solution.py:81
  370.9 55.5 %psum.15 = f32[4]{0:T(128)S(1)} all-reduce(f32[4]{0:T(128)S(1)} %get-tuple-element.430), channel_id=1, replica_groups=mesh['atoms'=32,'beads'=8] {'atoms'}, use_global_device_ids=true, to_apply=%region_18.19 | all-reduce | flops 4 | bytes 32 | tf_op jit(solution)/shard_map/psum | solution.py:145
  426.5 40.7 %while.65 = (s32[]{:T(128)}, f32[8,4,2,256]{3,2,1,0:T(2,128)S(1)}, f32[4,3,128]{2,0,1:T(4,128)S(1)}, f32[8,3,256]{2,1,0:T(4,128)S(1)}, f32[4,128]{1,0:T(4,128)S(1)}, /*index=5*/s32[]{:T(128)}, s32[]{:T(128)}, s32[]{}, s32[]{}) while((s32[]{:T(128)}, f32[8,4,2,256]{3,2,1,0:T(2,128)S(1)}, f32[4,3,128]{2,0,1:T(4,128)S(1)}, ...), condition=%wide.region_20.21_spmd, body=%wide.region_19.20_spmd.sunk | while | flops 4720644 | bytes 98437 | solution.py:67
  469.5 4.2 collective-permute-start.5
  473.6 54.2 %all-gather.8.cloned.1.call-done = f32[32,4,2,2048]{3,1,2,0:T(4,128)} async-done(((f32[1,4,2,2048]{3,1,2,0:T(4,128)}), f32[32,4,2,2048]{3,1,2,0:T(4,128)}) %all-gather.8.cloned.1.call-update) | async-done | bytes 2097168 | tf_op jit(solution)/shard_map/all_gather | solution.py:20
  529.9 26.1 %while.68 = (s32[]{:T(128)}, f32[4,3,128]{2,1,0:T(4,128)S(1)}, f32[8,3,256]{2,1,0:T(4,128)S(1)}, f32[4,3,128]{2,0,1:T(4,128)S(1)}, f32[8,4,2,256]{3,0,2,1:T(8,128)S(1)}, /*index=5*/s32[]{:T(128)}, s32[]{:T(128)}, s32[]{}, s32[]{}) while((s32[]{:T(128)}, f32[4,3,128]{2,1,0:T(4,128)S(1)}, f32[8,3,256]{2,1,0:T(4,128)S(1)}, ...), condition=%wide.region_23.24_spmd.clone, body=%wide.region_22.23_spmd.clone.sunk | while | flops 5901317 | bytes 103571 | solution.py:94
  530.0 3.1 fusion.222
  533.3 3.1 fusion.222
  536.5 3.1 fusion.222
  539.8 3.1 fusion.222
  543.1 3.1 fusion.222
  546.3 3.1 fusion.222
  549.6 3.1 fusion.222
  552.8 3.1 fusion.222
  (450 shorter events, 229.5 us)
Async XLA Ops:
  7.2 122.5 %all-gather.4.cloned.1.call-start = ((), (), s32[]{:S(2)}) async-start(), calls=%async_computation | async-start | bytes 2162688 | tf_op jit(solution)/shard_map/all_gather | solution.py:20
  8.0 54.8 %copy-start.6 = (f32[8]{0:T(128)S(1)}, f32[8]{0:T(128)}, u32[]{:S(2)}) copy-start(f32[8]{0:T(128)} %param.33) | copy-start | bytes 100
  8.0 54.8 %copy-start.7 = (s32[128]{0:T(128)S(1)}, s32[128]{0:T(128)}, u32[]{:S(2)}) copy-start(s32[128]{0:T(128)} %param.26) | copy-start | bytes 1540
  8.0 54.8 %copy-start.8 = (f32[8]{0:T(128)S(1)}, f32[8]{0:T(128)}, u32[]{:S(2)}) copy-start(f32[8]{0:T(128)} %param.31) | copy-start | bytes 100
  8.0 54.7 %copy-start.9 = (f32[8]{0:T(128)S(1)}, f32[8]{0:T(128)}, u32[]{:S(2)}) copy-start(f32[8]{0:T(128)} %param.32) | copy-start | bytes 100
  8.0 54.7 %copy-start.10 = (f32[8]{0:T(128)S(1)}, f32[8]{0:T(128)}, u32[]{:S(2)}) copy-start(f32[8]{0:T(128)} %param.30) | copy-start | bytes 100
  8.1 61.4 %copy-start.4 = (s32[8,128]{1,0:T(8,128)S(1)}, s32[8,128]{1,0:T(8,128)}, u32[]{:S(2)}) copy-start(s32[8,128]{1,0:T(8,128)} %param.27) | copy-start | bytes 12292
  8.1 61.4 %copy-start.2 = (f32[2048]{0:T(1024)S(1)}, f32[2048]{0:T(1024)}, u32[]{:S(2)}) copy-start(f32[2048]{0:T(1024)} %param.29) | copy-start | bytes 24580
  62.0 69.7 %copy-start = (f32[4,3,128]{2,0,1:T(4,128)S(1)}, f32[4,3,128]{2,0,1:T(4,128)}, u32[]{:S(2)}) copy-start(f32[4,3,128]{2,0,1:T(4,128)} %get-tuple-element.907) | copy-start | bytes 18436
  62.7 266.1 %all-gather.6.cloned.1.call-start = ((), (), s32[]{:S(2)}) async-start(), calls=%async_computation.1 | async-start | bytes 2162688 | tf_op jit(solution)/shard_map/all_gather | solution.py:20
  63.6 6.8 %collective-permute-start = (f32[4,32]{1,0:T(4,128)S(1)}, f32[4,32]{1,0:T(4,128)S(1)}, u32[]{:S(2)}, u32[]{:S(2)}) collective-permute-start(f32[4,32]{1,0:T(4,128)S(1)} %get-tuple-element.478), channel_id=1, source_target_pairs={{0,8},{8,16},{16,24},{24,32},{32,40},{40,48},{48,56},{56,64},{64,7... | collective-permute-start | bytes 1544 | tf_op jit(solution)/shard_map/ppermute | solution.py:31
  63.7 7.1 %collective-permute-start.1 = (f32[4,32]{1,0:T(4,128)S(1)}, f32[4,32]{1,0:T(4,128)S(1)}, u32[]{:S(2)}, u32[]{:S(2)}) collective-permute-start(f32[4,32]{1,0:T(4,128)S(1)} %get-tuple-element.479), channel_id=1, source_target_pairs={{8,0},{16,8},{24,16},{32,24},{40,32},{48,40},{56,48},{64,56},{72,6... | collective-permute-start | bytes 1544 | tf_op jit(solution)/shard_map/ppermute | solution.py:34
  131.7 40.0 %copy-start.1 = (f32[4,128]{1,0:T(4,128)S(1)}, f32[4,128]{1,0:T(4,128)}, u32[]{:S(2)}) copy-start(f32[4,128]{1,0:T(4,128)} %get-tuple-element.928) | copy-start | bytes 6148
  268.8 259.1 %all-gather.8.cloned.1.call-start = ((), (), s32[]{:S(2)}) async-start(), calls=%async_computation.2 | async-start | bytes 2162688 | tf_op jit(solution)/shard_map/all_gather | solution.py:20
  268.9 5.1 collective-permute-start.2
  269.0 5.2 collective-permute-start.3
  467.2 62.7 %copy-start.5 = (f32[4,128]{1,0:T(4,128)}, f32[4,128]{1,0:T(4,128)S(1)}, u32[]{:S(2)}) copy-start(f32[4,128]{1,0:T(4,128)S(1)} %get-tuple-element.933) | copy-start | bytes 6148
  467.9 88.1 %collective-permute-start.4 = (f32[1,3,128]{2,0,1:T(1,128)S(1)}, f32[1,3,128]{2,0,1:T(1,128)S(1)}, u32[]{:S(2)}, u32[]{:S(2)}) collective-permute-start(f32[1,3,128]{2,0,1:T(1,128)S(1)} %get-tuple-element.474), channel_id=1, source_target_pairs={{0,1},{1,2},{2,3},{3,4},{4,5},{5,6},{6,7},{7,0},{8,9},{9,10},{10,1... | collective-permute-start | bytes 4616 | tf_op jit(solution)/shard_map/ppermute | solution.py:31
  469.5 86.6 %collective-permute-start.5 = (f32[1,3,128]{2,0,1:T(1,128)S(1)}, f32[1,3,128]{2,0,1:T(1,128)S(1)}, u32[]{:S(2)}, u32[]{:S(2)}) collective-permute-start(f32[1,3,128]{2,0,1:T(1,128)S(1)} %get-tuple-element.475), channel_id=1, source_target_pairs={{1,0},{2,1},{3,2},{4,3},{5,4},{6,5},{7,6},{0,7},{9,8},{10,9},{11,1... | collective-permute-start | bytes 4616 | tf_op jit(solution)/shard_map/ppermute | solution.py:34
  529.9 26.1 %copy-start.3 = (f32[4,3,128]{2,0,1:T(4,128)S(1)}, f32[4,3,128]{2,0,1:T(4,128)}, u32[]{:S(2)}) copy-start(f32[4,3,128]{2,0,1:T(4,128)} %param.24) | copy-start | bytes 18436
Sparse Core Ops, SparseCore 0:
  62.8 66.8 all-gather.3
  268.9 59.8 all-gather.5
  468.0 59.8 all-gather.7
